TPU v7x, 256 devices: a whole 4x4x8 slice. The times are simulated.
256 devices in a mesh: gx: 8 (over z_hi, core), gy: 4 (over y), gz: 8 (over z_lo, x).
Axes of the slice: x: 4, y: 4, z: 8 (z_hi: 4, z_lo: 2; z = z_hi * 2 + z_lo), core: 2. Of those that a mesh axis runs over, the one named last changes fastest.
Arguments:
- features: bfloat16 [32768, 512], P(('gx', 'gy', 'gz')), may hold values from -6 to 6
- halo_index: int32 [24576], P(('gx', 'gy', 'gz')), may hold values from 0 to 127
- edge_src: int32 [2048, 384], P(('gx', 'gy', 'gz')), may hold values from 0 to 2623
- edge_dst: int32 [2048, 384], P(('gx', 'gy', 'gz')), may hold values from 0 to 127
- edge_count: int32 [2048], P(('gx', 'gy', 'gz')), may hold values from 48 to 384, as said below
- edge_basis: bfloat16 [786432, 128], P(('gx', 'gy', 'gz')), may hold values from -6 to 6
- w_edge_in: bfloat16 [8, 1152, 1024], P('gz'), may hold values from -0.1875 to 0.1875
- w_edge_out: bfloat16 [8, 1024, 512], P('gz'), may hold values from -0.1875 to 0.1875
- w_update: bfloat16 [512, 512], replicated, may hold values from -0.25 to 0.25
Outputs:
- new_features: bfloat16 [32768, 512], P(('gx', 'gy', 'gz'))
- halo_next: bfloat16 [6656, 96, 512], P(('gx', 'gy', 'gz'))
Inputs may be any that keep to these rules, and one draw needn't show every extreme that they name: The first edge_count slots of a domain's 384 slots for a species pair are live; in every draw some species pair has all 384 slots live in every domain of one gz group.
All inputs are finite; a program needn't handle non-finite values.
Results may differ from a plain program's by a relative error of at most 0.0051.
Values may be sent and summed in bfloat16 or wider, within the bound.
No kernel may reach another device: no remote copies, remote signals or barrier semaphores. Data moves between devices by JAX's collectives and lax.ppermute only.
A program may use at most 128 MiB of HBM per device.

v0:
```python
import jax
import jax.numpy as jnp
from jax import lax
from jax.sharding import PartitionSpec as P


def extended(x, sides, width):
    for axis, dim in sides:
        count, length = (lax.axis_size(axis), x.shape[dim])
        up = [(i, (i + 1) % count) for i in range(count)]
        down = [(j, i) for i, j in up]
        last = lax.slice_in_dim(x, length - width, length, axis=dim)
        first = lax.slice_in_dim(x, 0, width, axis=dim)
        before = lax.ppermute(last, axis, up)
        after = lax.ppermute(first, axis, down)
        x = jnp.concatenate([before, x, after], axis=dim)
    return x


def in_order(tiles, dim):
    tiles = jnp.moveaxis(tiles, 0, dim)
    shape = tiles.shape
    return tiles.reshape(*shape[:dim], shape[dim] * shape[dim + 1], *shape[dim + 2 :])


def copy_for_each(x, axis):
    copies = jnp.broadcast_to(x, (lax.axis_size(axis), *x.shape))
    return lax.all_to_all(copies, axis, split_axis=0, concat_axis=0, tiled=True)


def gathered_copies(x, axis, dim):
    return in_order(copy_for_each(x, axis), dim)


def outer_cells(padded):
    flat = padded.reshape(27, padded.shape[3], padded.shape[4])
    return jnp.concatenate([flat[:13], flat[14:]], axis=0)


def shards(
    features,
    halo_index,
    edge_src,
    edge_dst,
    edge_count,
    edge_basis,
    w_edge_in,
    w_edge_out,
    w_update,
):
    model_width = features.shape[1]
    atom_count = features.shape[0]
    group_count = edge_src.shape[0]
    slot_count = edge_src.shape[1]
    first_layer = w_edge_in[0]
    w_source = first_layer[:model_width]
    w_target = first_layer[model_width : 2 * model_width]
    w_radial = first_layer[2 * model_width :]
    w_second = w_edge_out[0]
    boundary = features[halo_index]
    padded = extended(boundary[None, None, None], (("gx", 0), ("gy", 1), ("gz", 2)), 1)
    table_rows = jnp.concatenate([features, outer_cells(padded).reshape(-1, model_width)], axis=0)
    slot_index = lax.broadcasted_iota(jnp.int32, (group_count, slot_count), 1)
    dst_live = jnp.where(slot_index < edge_count[:, None], edge_dst, -1)
    src_rows = table_rows[edge_src]
    basis_rows = edge_basis.reshape(group_count, slot_count, -1)
    owners = gathered_copies(features, "gz", 0)
    source_part = lax.all_to_all(src_rows, "gz", split_axis=0, concat_axis=0, tiled=True)
    radial_part = lax.all_to_all(basis_rows, "gz", split_axis=0, concat_axis=0, tiled=True)
    target_part = lax.all_to_all(dst_live, "gz", split_axis=0, concat_axis=0, tiled=True)
    owner_index = lax.broadcasted_iota(jnp.int32, target_part.shape, 0)
    row_index = owner_index * atom_count + jnp.maximum(target_part, 0)
    pre = jnp.einsum("ock,kh->och", source_part, w_source, preferred_element_type=jnp.float32)
    pre = pre + jnp.einsum(
        "ock,kh->och", owners[row_index], w_target, preferred_element_type=jnp.float32
    )
    pre = pre + jnp.einsum("ock,kh->och", radial_part, w_radial, preferred_element_type=jnp.float32)
    hidden = jax.nn.silu(pre).astype(jnp.bfloat16)
    messages = jnp.einsum(
        "och,hd->ocd", hidden, w_second, preferred_element_type=jnp.float32
    ).astype(jnp.bfloat16)
    atom_iota = lax.broadcasted_iota(jnp.int32, (1, atom_count, 1), 1)
    incidence = (target_part[:, None, :] == atom_iota).astype(jnp.bfloat16)
    partial_value = jnp.einsum(
        "oac,ocd->oad", incidence, messages, preferred_element_type=jnp.float32
    )
    returned = lax.all_to_all(partial_value, "gz", split_axis=0, concat_axis=0, tiled=True)
    summed = jnp.sum(returned, axis=0)
    mean_square = jnp.mean(summed * summed, axis=-1, keepdims=True)
    normed = (summed * lax.rsqrt(mean_square + 1e-05)).astype(jnp.bfloat16)
    update = jnp.dot(normed, w_update, preferred_element_type=jnp.float32)
    new_rows = (features.astype(jnp.float32) + update).astype(jnp.bfloat16)
    boundary_next = new_rows[halo_index]
    padded_next = extended(boundary_next[None, None, None], (("gx", 0), ("gy", 1), ("gz", 2)), 1)
    return (new_rows, outer_cells(padded_next))


def solution(mesh):
    in_specs = (
        P(("gx", "gy", "gz"), None),
        P(("gx", "gy", "gz")),
        P(("gx", "gy", "gz"), None),
        P(("gx", "gy", "gz"), None),
        P(("gx", "gy", "gz")),
        P(("gx", "gy", "gz"), None),
        P("gz", None, None),
        P("gz", None, None),
        P(),
    )
    out_specs = (P(("gx", "gy", "gz"), None), P(("gx", "gy", "gz"), None, None))
    return jax.shard_map(shards, mesh=mesh, in_specs=in_specs, out_specs=out_specs, check_vma=False)
```

profile of v0, /device:TPU:1, one launch (start us, length us, event | category | flops | bytes accessed | tf_op | source)
XLA Modules:
  0.0 239.3 jit_solution(6558836597803333501)
XLA Ops:
  3.2 3.3 %collective-permute-start.1 = (bf16[1,1,1,96,512]{4,3,2,1,0:T(8,128)(2,1)S(1)}, bf16[1,1,1,96,512]{4,3,2,1,0:T(8,128)(2,1)S(1)}, u32[]{:S(2)}, u32[]{:S(2)}) collective-permute-start(bf16[1,1,1,96,512]{4,3,2,1,0:T(8,128)(2,1)S(1)} %bitcast.45), channel_id=1, source_target_pairs={{32,0},{64,32},{96,64},{128,96},{160,128},{192,160},{224,192},{0,2... | collective-permute-start | bytes 294920 | tf_op jit(solution)/shard_map/ppermute | solution.py:15
  7.7 2.2 collective-permute-done.1
  11.3 2.8 %collective-permute-start.3 = (bf16[3,1,1,96,512]{4,3,2,1,0:T(8,128)(2,1)S(1)}, bf16[3,1,1,96,512]{4,3,2,1,0:T(8,128)(2,1)S(1)}, u32[]{:S(2)}, u32[]{:S(2)}) collective-permute-start(bf16[3,1,1,96,512]{4,3,2,1,0:T(8,128)(2,1)S(1)} %pad_maximum_fusion.7), channel_id=1, source_target_pairs={{8,0},{16,8},{24,16},{0,24},{9,1},{17,9},{25,17},{1,25},{10,2},{18... | collective-permute-start | bytes 884744 | tf_op jit(solution)/shard_map/ppermute | solution.py:15
  14.1 3.7 %collective-permute-done.3 = bf16[3,1,1,96,512]{4,3,2,1,0:T(8,128)(2,1)S(1)} collective-permute-done((bf16[3,1,1,96,512]{4,3,2,1,0:T(8,128)(2,1)S(1)}, bf16[3,1,1,96,512]{4,3,2,1,0:T(8,128)(2,1)S(1)}, u32[]{:S(2)}, u32[]{:S(2)}) %collective-permute-start.3) | collective-permute-done | bytes 294944 | tf_op jit(solution)/shard_map/ppermute | solution.py:15
  17.8 3.1 %collective-permute-done.2 = bf16[3,1,1,96,512]{4,3,2,1,0:T(8,128)(2,1)S(1)} collective-permute-done((bf16[3,1,1,96,512]{4,3,2,1,0:T(8,128)(2,1)S(1)}, bf16[3,1,1,96,512]{4,3,2,1,0:T(8,128)(2,1)S(1)}, u32[]{:S(2)}, u32[]{:S(2)}) %collective-permute-start.2) | collective-permute-done | bytes 294944 | tf_op jit(solution)/shard_map/ppermute | solution.py:14
  21.9 2.9 %collective-permute-start.5 = (bf16[3,3,1,96,512]{4,3,2,1,0:T(8,128)(2,1)}, bf16[3,3,1,96,512]{4,3,2,1,0:T(8,128)(2,1)}, u32[]{:S(2)}, u32[]{:S(2)}) collective-permute-start(bf16[3,3,1,96,512]{4,3,2,1,0:T(8,128)(2,1)} %pad_maximum_fusion.5), channel_id=1, source_target_pairs={{1,0},{2,1},{3,2},{4,3},{5,4},{6,5},{7,6},{0,7},{9,8},{10,9},{11,1... | collective-permute-start | bytes 2654216 | tf_op jit(solution)/shard_map/ppermute | solution.py:15
  25.0 15.4 %all_to_all.29 = s32[8,1,384]{2,1,0:T(1,128)S(1)} all-to-all(s32[8,1,384]{2,1,0:T(1,128)S(1)} %all_to_all.18), channel_id=1, replica_groups=mesh['gx'=8,'gy'=4,'gz'=8] {'gz'}, dimensions={0} | all-to-all | bytes 24576 | tf_op jit(solution)/shard_map/all_to_all | solution.py:70
  41.5 3.6 %all-to-all-start.2 = ((bf16[8,128,512]{2,1,0:T(8,128)(2,1)}), bf16[8,128,512]{2,1,0:T(8,128)(2,1)S(1)}, u32[]{:S(2)}, u32[]{:S(2)}) async-start(bf16[8,128,512]{2,1,0:T(8,128)(2,1)} %broadcast_in_dim.28), calls=%async_computation.2 | async-start | bytes 2097152 | tf_op jit(solution)/shard_map/all_to_all | solution.py:28
  48.9 15.5 %gather_fusion.1 = bf16[3072,512]{1,0:T(8,128)(2,1)} fusion(bf16[2624,512]{1,0:T(8,128)(2,1)} %pad_maximum_fusion, s32[3072]{0:T(1024)S(1)} %broadcast_clamp_fusion.1), kind=kCustom, calls=%fused_computation.1 | custom fusion | bytes 6303744 | tf_op jit(solution)/shard_map/gather | solution.py:65
  64.3 5.1 %all-to-all-start.1 = ((bf16[8,384,512]{2,1,0:T(8,128)(2,1)}), bf16[8,384,512]{2,1,0:T(8,128)(2,1)}, u32[]{:S(2)}, u32[]{:S(2)}) async-start(bf16[8,384,512]{2,1,0:T(8,128)(2,1)} %bitcast.40), calls=%async_computation.1 | async-start | bytes 6291456 | tf_op jit(solution)/shard_map/all_to_all | solution.py:68
  69.5 36.4 %all-to-all-done.1 = bf16[8,384,512]{2,1,0:T(8,128)(2,1)} async-done(((bf16[8,384,512]{2,1,0:T(8,128)(2,1)}), bf16[8,384,512]{2,1,0:T(8,128)(2,1)}, u32[]{:S(2)}, u32[]{:S(2)}) %all-to-all-start.1) | async-done | bytes 3145760 | tf_op jit(solution)/shard_map/all_to_all | solution.py:68
  105.9 3.9 %all-to-all-start.3 = ((bf16[8,384,128]{2,1,0:T(8,128)(2,1)}), bf16[8,384,128]{2,1,0:T(8,128)(2,1)S(1)}, u32[]{:S(2)}, u32[]{:S(2)}) async-start(bf16[8,384,128]{2,1,0:T(8,128)(2,1)} %bitcast.12), calls=%async_computation.3 | async-start | bytes 1572864 | tf_op jit(solution)/shard_map/all_to_all | solution.py:69
  109.8 13.3 %gather_fusion.2 = bf16[3072,512]{1,0:T(8,128)(2,1)} fusion(bf16[1024,512]{1,0:T(8,128)(2,1)S(1)} %bitcast.39, s32[3072]{0:T(1024)S(1)} %broadcast_clamp_fusion), kind=kCustom, calls=%fused_computation.2 | custom fusion | bytes 6303744 | tf_op jit(solution)/shard_map/gather | solution.py:75
  123.1 10.1 %fusion.7 = f32[8,384,1024]{2,1,0:T(8,128)} fusion(bf16[8,384,512]{2,1,0:T(8,128)(2,1)} %bitcast.44, bf16[1,1152,1024]{2,1,0:T(8,128)(2,1)} %param.15), kind=kOutput, calls=%fused_computation.18 | convolution fusion | flops 3221225472 | bytes 16777216 | tf_op jit(solution)/shard_map/ock,kh->och/dot_general | solution.py:74
  133.2 10.1 %fusion.9 = f32[8,384,1024]{2,1,0:T(8,128)} fusion(bf16[8,384,512]{2,1,0:T(8,128)(2,1)} %all-to-all-done.1, bf16[1,1152,1024]{2,1,0:T(8,128)(2,1)} %param.15), kind=kOutput, calls=%fused_computation.20 | convolution fusion | flops 3221225472 | bytes 16777216 | tf_op jit(solution)/shard_map/ock,kh->och/dot_general | solution.py:73
  143.3 12.7 %fusion = bf16[8,384,512]{2,1,0:T(8,128)(2,1)} fusion(f32[8,384,1024]{2,1,0:T(8,128)} %fusion.9, f32[8,384,1024]{2,1,0:T(8,128)} %fusion.7, bf16[8,384,128]{2,1,0:T(8,128)(2,1)S(1)} %all-to-all-done.3, bf16[1,1024,512]{2,1,0:T(8,128)(2,1)S(1)} %copy-done, bf16[1,1152,1024]{2,1,0:T(8,128)(2,1)} %param.15), kind=kOutput, calls=%fused_computation.5 | convolution fusion | flops 4048551936 | bytes 30408704 | tf_op jit(solution)/shard_map/och,hd->ocd/dot_general | solution.py:79
  156.0 2.6 %fusion.3 = f32[8,128,512]{2,1,0:T(8,128)S(1)} fusion(bf16[8,384,512]{2,1,0:T(8,128)(2,1)} %fusion, s32[8,384]{1,0:T(8,128)S(1)} %bitcast.56), kind=kOutput, calls=%fused_computation.7 | convolution fusion | flops 403046400 | bytes 5255168 | tf_op jit(solution)/shard_map/oac,ocd->oad/dot_general | solution.py:84
  158.7 29.4 %all_to_all.30 = f32[8,128,512]{2,1,0:T(8,128)S(1)} all-to-all(f32[8,128,512]{2,1,0:T(8,128)S(1)} %fusion.3), channel_id=1, replica_groups=mesh['gx'=8,'gy'=4,'gz'=8] {'gz'}, dimensions={0} | all-to-all | bytes 4194304 | tf_op jit(solution)/shard_map/all_to_all | solution.py:87
  189.5 3.8 %collective-permute-start.7 = (bf16[1,1,1,96,512]{4,3,2,1,0:T(8,128)(2,1)S(1)}, bf16[1,1,1,96,512]{4,3,2,1,0:T(8,128)(2,1)S(1)}, u32[]{:S(2)}, u32[]{:S(2)}) collective-permute-start(bf16[1,1,1,96,512]{4,3,2,1,0:T(8,128)(2,1)S(1)} %bitcast.50), channel_id=1, source_target_pairs={{32,0},{64,32},{96,64},{128,96},{160,128},{192,160},{224,192},{0,2... | collective-permute-start | bytes 294920 | tf_op jit(solution)/shard_map/ppermute | solution.py:15
  193.3 14.1 %collective-permute-start.6 = (bf16[1,1,1,96,512]{4,3,2,1,0:T(8,128)(2,1)S(1)}, bf16[1,1,1,96,512]{4,3,2,1,0:T(8,128)(2,1)S(1)}, u32[]{:S(2)}, u32[]{:S(2)}) collective-permute-start(bf16[1,1,1,96,512]{4,3,2,1,0:T(8,128)(2,1)S(1)} %bitcast.51), channel_id=1, source_target_pairs={{0,32},{32,64},{64,96},{96,128},{128,160},{160,192},{192,224},{224... | collective-permute-start | bytes 294920 | tf_op jit(solution)/shard_map/ppermute | solution.py:14
  207.5 3.3 %collective-permute-done.7 = bf16[1,1,1,96,512]{4,3,2,1,0:T(8,128)(2,1)S(1)} collective-permute-done((bf16[1,1,1,96,512]{4,3,2,1,0:T(8,128)(2,1)S(1)}, bf16[1,1,1,96,512]{4,3,2,1,0:T(8,128)(2,1)S(1)}, u32[]{:S(2)}, u32[]{:S(2)}) %collective-permute-start.7) | collective-permute-done | bytes 98336 | tf_op jit(solution)/shard_map/ppermute | solution.py:15
  212.4 4.6 %collective-permute-done.9 = bf16[3,1,1,96,512]{4,3,2,1,0:T(8,128)(2,1)S(1)} collective-permute-done((bf16[3,1,1,96,512]{4,3,2,1,0:T(8,128)(2,1)S(1)}, bf16[3,1,1,96,512]{4,3,2,1,0:T(8,128)(2,1)S(1)}, u32[]{:S(2)}, u32[]{:S(2)}) %collective-permute-start.9) | collective-permute-done | bytes 294944 | tf_op jit(solution)/shard_map/ppermute | solution.py:15
  219.5 15.2 %collective-permute-done.11 = bf16[3,3,1,96,512]{4,3,2,1,0:T(8,128)(2,1)S(1)} collective-permute-done((bf16[3,3,1,96,512]{4,3,2,1,0:T(8,128)(2,1)S(1)}, bf16[3,3,1,96,512]{4,3,2,1,0:T(8,128)(2,1)S(1)}, u32[]{:S(2)}, u32[]{:S(2)}) %collective-permute-start.11) | collective-permute-done | bytes 884768 | tf_op jit(solution)/shard_map/ppermute | solution.py:15
  234.7 2.4 %collective-permute-done.10 = bf16[3,3,1,96,512]{4,3,2,1,0:T(8,128)(2,1)S(1)} collective-permute-done((bf16[3,3,1,96,512]{4,3,2,1,0:T(8,128)(2,1)S(1)}, bf16[3,3,1,96,512]{4,3,2,1,0:T(8,128)(2,1)S(1)}, u32[]{:S(2)}, u32[]{:S(2)}) %collective-permute-start.10) | collective-permute-done | bytes 884768 | tf_op jit(solution)/shard_map/ppermute | solution.py:14
  (59 shorter events, 18.8 us)
Async XLA Ops:
  0.6 142.7 %copy-start = (bf16[1,1024,512]{2,1,0:T(8,128)(2,1)S(1)}, bf16[1,1024,512]{2,1,0:T(8,128)(2,1)}, u32[]{:S(2)}) copy-start(bf16[1,1024,512]{2,1,0:T(8,128)(2,1)} %param.16) | copy-start | bytes 3145732
  0.6 39.8 %copy-start.2 = (bf16[128,512]{1,0:T(8,128)(2,1)S(1)}, bf16[128,512]{1,0:T(8,128)(2,1)}, u32[]{:S(2)}) copy-start(bf16[128,512]{1,0:T(8,128)(2,1)} %param.9) | copy-start | bytes 393220
  0.7 24.2 %copy-start.7 = (s32[8]{0:T(128)S(1)}, s32[8]{0:T(128)}, u32[]{:S(2)}) copy-start(s32[8]{0:T(128)} %param.13) | copy-start | bytes 100
  0.7 24.2 %copy-start.5 = (s32[8,384]{1,0:T(8,128)S(1)}, s32[8,384]{1,0:T(8,128)}, u32[]{:S(2)}) copy-start(s32[8,384]{1,0:T(8,128)} %param.12) | copy-start | bytes 36868
  3.2 6.8 %collective-permute-start.1 = (bf16[1,1,1,96,512]{4,3,2,1,0:T(8,128)(2,1)S(1)}, bf16[1,1,1,96,512]{4,3,2,1,0:T(8,128)(2,1)S(1)}, u32[]{:S(2)}, u32[]{:S(2)}) collective-permute-start(bf16[1,1,1,96,512]{4,3,2,1,0:T(8,128)(2,1)S(1)} %bitcast.45), channel_id=1, source_target_pairs={{32,0},{64,32},{96,64},{128,96},{160,128},{192,160},{224,192},{0,2... | collective-permute-start | bytes 294920 | tf_op jit(solution)/shard_map/ppermute | solution.py:15
  6.5 4.8 %collective-permute-start = (bf16[1,1,1,96,512]{4,3,2,1,0:T(8,128)(2,1)S(1)}, bf16[1,1,1,96,512]{4,3,2,1,0:T(8,128)(2,1)S(1)}, u32[]{:S(2)}, u32[]{:S(2)}) collective-permute-start(bf16[1,1,1,96,512]{4,3,2,1,0:T(8,128)(2,1)S(1)} %bitcast.46), channel_id=1, source_target_pairs={{0,32},{32,64},{64,96},{96,128},{128,160},{160,192},{192,224},{224... | collective-permute-start | bytes 294920 | tf_op jit(solution)/shard_map/ppermute | solution.py:14
  11.3 33.7 %copy-start.6 = (s32[8,384]{1,0:T(8,128)S(1)}, s32[8,384]{1,0:T(8,128)}, u32[]{:S(2)}) copy-start(s32[8,384]{1,0:T(8,128)} %param.11) | copy-start | bytes 36868
  11.3 6.5 %collective-permute-start.3 = (bf16[3,1,1,96,512]{4,3,2,1,0:T(8,128)(2,1)S(1)}, bf16[3,1,1,96,512]{4,3,2,1,0:T(8,128)(2,1)S(1)}, u32[]{:S(2)}, u32[]{:S(2)}) collective-permute-start(bf16[3,1,1,96,512]{4,3,2,1,0:T(8,128)(2,1)S(1)} %pad_maximum_fusion.7), channel_id=1, source_target_pairs={{8,0},{16,8},{24,16},{0,24},{9,1},{17,9},{25,17},{1,25},{10,2},{18... | collective-permute-start | bytes 884744 | tf_op jit(solution)/shard_map/ppermute | solution.py:15
  14.1 6.8 %collective-permute-start.2 = (bf16[3,1,1,96,512]{4,3,2,1,0:T(8,128)(2,1)S(1)}, bf16[3,1,1,96,512]{4,3,2,1,0:T(8,128)(2,1)S(1)}, u32[]{:S(2)}, u32[]{:S(2)}) collective-permute-start(bf16[3,1,1,96,512]{4,3,2,1,0:T(8,128)(2,1)S(1)} %pad_maximum_fusion.7), channel_id=1, source_target_pairs={{0,8},{8,16},{16,24},{24,0},{1,9},{9,17},{17,25},{25,1},{2,10},{10... | collective-permute-start | bytes 884744 | tf_op jit(solution)/shard_map/ppermute | solution.py:14
  21.9 23.2 %collective-permute-start.5 = (bf16[3,3,1,96,512]{4,3,2,1,0:T(8,128)(2,1)}, bf16[3,3,1,96,512]{4,3,2,1,0:T(8,128)(2,1)}, u32[]{:S(2)}, u32[]{:S(2)}) collective-permute-start(bf16[3,3,1,96,512]{4,3,2,1,0:T(8,128)(2,1)} %pad_maximum_fusion.5), channel_id=1, source_target_pairs={{1,0},{2,1},{3,2},{4,3},{5,4},{6,5},{7,6},{0,7},{9,8},{10,9},{11,1... | collective-permute-start | bytes 2654216 | tf_op jit(solution)/shard_map/ppermute | solution.py:15
  24.9 20.2 %collective-permute-start.4 = (bf16[3,3,1,96,512]{4,3,2,1,0:T(8,128)(2,1)}, bf16[3,3,1,96,512]{4,3,2,1,0:T(8,128)(2,1)}, u32[]{:S(2)}, u32[]{:S(2)}) collective-permute-start(bf16[3,3,1,96,512]{4,3,2,1,0:T(8,128)(2,1)} %pad_maximum_fusion.5), channel_id=1, source_target_pairs={{0,1},{1,2},{2,3},{3,4},{4,5},{5,6},{6,7},{7,0},{8,9},{9,10},{10,1... | collective-permute-start | bytes 2654216 | tf_op jit(solution)/shard_map/ppermute | solution.py:14
  41.5 22.8 %all-to-all-start.2 = ((bf16[8,128,512]{2,1,0:T(8,128)(2,1)}), bf16[8,128,512]{2,1,0:T(8,128)(2,1)S(1)}, u32[]{:S(2)}, u32[]{:S(2)}) async-start(bf16[8,128,512]{2,1,0:T(8,128)(2,1)} %broadcast_in_dim.28), calls=%async_computation.2 | async-start | bytes 2097152 | tf_op jit(solution)/shard_map/all_to_all | solution.py:28
  64.3 41.5 %all-to-all-start.1 = ((bf16[8,384,512]{2,1,0:T(8,128)(2,1)}), bf16[8,384,512]{2,1,0:T(8,128)(2,1)}, u32[]{:S(2)}, u32[]{:S(2)}) async-start(bf16[8,384,512]{2,1,0:T(8,128)(2,1)} %bitcast.40), calls=%async_computation.1 | async-start | bytes 6291456 | tf_op jit(solution)/shard_map/all_to_all | solution.py:68
  105.9 37.5 %all-to-all-start.3 = ((bf16[8,384,128]{2,1,0:T(8,128)(2,1)}), bf16[8,384,128]{2,1,0:T(8,128)(2,1)S(1)}, u32[]{:S(2)}, u32[]{:S(2)}) async-start(bf16[8,384,128]{2,1,0:T(8,128)(2,1)} %bitcast.12), calls=%async_computation.3 | async-start | bytes 1572864 | tf_op jit(solution)/shard_map/all_to_all | solution.py:69
  158.7 29.8 %copy-start.4 = (bf16[512,512]{1,0:T(8,128)(2,1)S(1)}, bf16[512,512]{1,0:T(8,128)(2,1)}, u32[]{:S(2)}) copy-start(bf16[512,512]{1,0:T(8,128)(2,1)} %param.17) | copy-start | bytes 1572868
  188.7 48.7 %copy-start.3 = (bf16[128,512]{1,0:T(8,128)(2,1)}, bf16[128,512]{1,0:T(8,128)(2,1)S(1)}, u32[]{:S(2)}) copy-start(bf16[128,512]{1,0:T(8,128)(2,1)S(1)} %fusion.5) | copy-start | bytes 393220
  189.5 21.3 %collective-permute-start.7 = (bf16[1,1,1,96,512]{4,3,2,1,0:T(8,128)(2,1)S(1)}, bf16[1,1,1,96,512]{4,3,2,1,0:T(8,128)(2,1)S(1)}, u32[]{:S(2)}, u32[]{:S(2)}) collective-permute-start(bf16[1,1,1,96,512]{4,3,2,1,0:T(8,128)(2,1)S(1)} %bitcast.50), channel_id=1, source_target_pairs={{32,0},{64,32},{96,64},{128,96},{160,128},{192,160},{224,192},{0,2... | collective-permute-start | bytes 294920 | tf_op jit(solution)/shard_map/ppermute | solution.py:15
  193.3 17.5 %collective-permute-start.6 = (bf16[1,1,1,96,512]{4,3,2,1,0:T(8,128)(2,1)S(1)}, bf16[1,1,1,96,512]{4,3,2,1,0:T(8,128)(2,1)S(1)}, u32[]{:S(2)}, u32[]{:S(2)}) collective-permute-start(bf16[1,1,1,96,512]{4,3,2,1,0:T(8,128)(2,1)S(1)} %bitcast.51), channel_id=1, source_target_pairs={{0,32},{32,64},{64,96},{96,128},{128,160},{160,192},{192,224},{224... | collective-permute-start | bytes 294920 | tf_op jit(solution)/shard_map/ppermute | solution.py:14
  210.9 6.1 %collective-permute-start.9 = (bf16[3,1,1,96,512]{4,3,2,1,0:T(8,128)(2,1)S(1)}, bf16[3,1,1,96,512]{4,3,2,1,0:T(8,128)(2,1)S(1)}, u32[]{:S(2)}, u32[]{:S(2)}) collective-permute-start(bf16[3,1,1,96,512]{4,3,2,1,0:T(8,128)(2,1)S(1)} %pad_maximum_fusion.8), channel_id=1, source_target_pairs={{8,0},{16,8},{24,16},{0,24},{9,1},{17,9},{25,17},{1,25},{10,2},{18... | collective-permute-start | bytes 884744 | tf_op jit(solution)/shard_map/ppermute | solution.py:15
  211.1 6.8 %collective-permute-start.8 = (bf16[3,1,1,96,512]{4,3,2,1,0:T(8,128)(2,1)S(1)}, bf16[3,1,1,96,512]{4,3,2,1,0:T(8,128)(2,1)S(1)}, u32[]{:S(2)}, u32[]{:S(2)}) collective-permute-start(bf16[3,1,1,96,512]{4,3,2,1,0:T(8,128)(2,1)S(1)} %pad_maximum_fusion.8), channel_id=1, source_target_pairs={{0,8},{8,16},{16,24},{24,0},{1,9},{9,17},{17,25},{25,1},{2,10},{10... | collective-permute-start | bytes 884744 | tf_op jit(solution)/shard_map/ppermute | solution.py:14
  218.0 16.7 %collective-permute-start.11 = (bf16[3,3,1,96,512]{4,3,2,1,0:T(8,128)(2,1)S(1)}, bf16[3,3,1,96,512]{4,3,2,1,0:T(8,128)(2,1)S(1)}, u32[]{:S(2)}, u32[]{:S(2)}) collective-permute-start(bf16[3,3,1,96,512]{4,3,2,1,0:T(8,128)(2,1)S(1)} %pad_maximum_fusion.6), channel_id=1, source_target_pairs={{1,0},{2,1},{3,2},{4,3},{5,4},{6,5},{7,6},{0,7},{9,8},{10,9},{11,1... | collective-permute-start | bytes 2654216 | tf_op jit(solution)/shard_map/ppermute | solution.py:15
  219.3 17.8 %collective-permute-start.10 = (bf16[3,3,1,96,512]{4,3,2,1,0:T(8,128)(2,1)S(1)}, bf16[3,3,1,96,512]{4,3,2,1,0:T(8,128)(2,1)S(1)}, u32[]{:S(2)}, u32[]{:S(2)}) collective-permute-start(bf16[3,3,1,96,512]{4,3,2,1,0:T(8,128)(2,1)S(1)} %pad_maximum_fusion.6), channel_id=1, source_target_pairs={{0,1},{1,2},{2,3},{3,4},{4,5},{5,6},{6,7},{7,0},{8,9},{9,10},{10,1... | collective-permute-start | bytes 2654216 | tf_op jit(solution)/shard_map/ppermute | solution.py:14
  237.5 1.9 copy-start.1
where the time goes:
time: 244 us; the launch traced here: 239 us
  waiting for transfers between devices  73.1 us (30%)
  blocking collectives  44.8 us (18%)
  starting transfers between devices  43.9 us (18%)
  matrix products  35.8 us (15%)
  local copies, waits for them, and re-layouts  32.7 us (13%)
  other arithmetic  8.03 us (3%)
    all_to_all x1, waiting for transfers between devices, shards(): lax.all_to_all(src_rows, 'gz', split_axis=0, concat_axis=0, tiled=True)  36.4 us
    all_to_all x1, blocking collectives, shards(): lax.all_to_all(partial_value, 'gz', split_axis=0, concat_axis=0, tiled=True)  29.4 us
    ppermute x6, waiting for transfers between devices, extended(): after = lax.ppermute(first, axis, down)  28.9 us
    ppermute x6, starting transfers between devices, extended(): before = lax.ppermute(last, axis, up)  16.9 us
    gather x1, local copies, waits for them, and re-layouts, shards(): src_rows = table_rows[edge_src]  15.5 us
    all_to_all x1, blocking collectives, shards(): lax.all_to_all(dst_live, 'gz', split_axis=0, concat_axis=0, tiled=True)  15.4 us
    ppermute x6, starting transfers between devices, extended(): after = lax.ppermute(first, axis, down)  14.4 us
    gather x1, local copies, waits for them, and re-layouts, shards(): owners[row_index]  13.3 us
  transfers between devices with their start and end apart: 15, of which 10 were waited for; matrix products, arithmetic and copies ran while one was open for 23% of the time, Pallas kernels for 0%

commit v1 on v0

v1 whole, which is shorter than its diff:
```python
import functools

import jax
import jax.numpy as jnp
from jax import lax
from jax.experimental import pallas as pl
from jax.experimental.pallas import tpu as pltpu
from jax.sharding import PartitionSpec as P

PIECES = 9
VMEM_BYTES = 56 * 1024 * 1024


def ring(axis, step):
    count = lax.axis_size(axis)
    return [(i, (i + step) % count) for i in range(count)]


def from_before(x, axis):
    return lax.ppermute(x, axis, ring(axis, 1))


def from_after(x, axis):
    return lax.ppermute(x, axis, ring(axis, -1))


def inner_swap(x):
    count = lax.axis_size("gx")
    return lax.ppermute(x, "gx", [(i, i ^ 1) for i in range(count)])


def outer_swap(x):
    count = lax.axis_size("gx")
    pairs = [(i, (i + 1) % count if i % 2 else (i - 1) % count) for i in range(count)]
    return lax.ppermute(x, "gx", pairs)


def halo_pieces(block):
    own = jnp.stack([from_before(block, "gz"), block, from_after(block, "gz")])
    outer = outer_swap(own)
    before, after = from_before(own, "gy"), from_after(own, "gy")
    inner = inner_swap(own)
    outer_before, outer_after = from_before(outer, "gy"), from_after(outer, "gy")
    inner_before, inner_after = inner_swap(before), inner_swap(after)
    return (
        own, before, after,
        outer, outer_before, outer_after,
        inner, inner_before, inner_after,
    )


def table_row(edge_src, atom_count, halo_count, odd):
    outside = jnp.maximum(edge_src - atom_count, 0)
    k = outside // halo_count
    row = outside - k * halo_count
    cell = k + (k >= 13)
    a, b, c = cell // 9, (cell // 3) % 3, cell % 3
    column = jnp.where(a == 1, 0, jnp.where((a == 0) != odd, 1, 2))
    turn = jnp.where(b == 1, 0, jnp.where(b == 0, 1, 2))
    there = atom_count + ((column * 3 + turn) * 3 + c) * halo_count + row
    return jnp.where(edge_src < atom_count, edge_src, there)


def gather_kernel(index_ref, features_ref, *refs):
    pieces, (out_ref, table, picks, sems) = refs[:PIECES], refs[PIECES:]
    atoms = features_ref.shape[0]
    span = pieces[0].shape[0]
    used = atoms + PIECES * span
    slots = index_ref.shape[2]

    @pl.when(pl.program_id(0) == 0)
    def _():
        copies = [pltpu.make_async_copy(features_ref, table.at[pl.ds(0, atoms)], sems.at[0])]
        for n, piece in enumerate(pieces):
            where = table.at[pl.ds(atoms + n * span, span)]
            copies.append(pltpu.make_async_copy(piece, where, sems.at[n + 1]))
        for copy in copies:
            copy.start()
        table[pl.ds(used, table.shape[0] - used), :] = jnp.zeros(
            (table.shape[0] - used, table.shape[1]), table.dtype
        )
        for copy in copies:
            copy.wait()

    wide = lax.transpose(jnp.broadcast_to(index_ref[0], (128, slots)), (1, 0))
    lanes = lax.broadcasted_iota(jnp.int32, (slots, 128), 1)
    for n in range(table.shape[0] // 128):
        hit = wide == lanes + n * 128
        picks[:, n * 128 : (n + 1) * 128] = jnp.where(hit, 1.0, 0.0).astype(picks.dtype)
    out_ref[0] = jnp.dot(picks[...], table[...], preferred_element_type=jnp.float32).astype(
        out_ref.dtype
    )


def gather_rows(index, features, pieces):
    groups, slots = index.shape
    atoms, width = features.shape
    pieces = [piece.reshape(-1, width) for piece in pieces]
    rows = -(-(atoms + PIECES * pieces[0].shape[0]) // 256) * 256
    anywhere = pl.BlockSpec(memory_space=pl.ANY)
    return pl.pallas_call(
        gather_kernel,
        grid=(groups,),
        in_specs=[pl.BlockSpec((1, 1, slots), lambda g: (g, 0, 0))] + [anywhere] * (1 + PIECES),
        out_specs=pl.BlockSpec((1, slots, width), lambda g: (g, 0, 0)),
        out_shape=jax.ShapeDtypeStruct((groups, slots, width), features.dtype),
        scratch_shapes=[
            pltpu.VMEM((rows, width), features.dtype),
            pltpu.VMEM((slots, rows), features.dtype),
            pltpu.SemaphoreType.DMA((1 + PIECES,)),
        ],
        compiler_params=pltpu.CompilerParams(vmem_limit_bytes=VMEM_BYTES),
        cost_estimate=pl.CostEstimate(
            flops=2 * groups * slots * rows * width,
            bytes_accessed=2 * width * (rows + groups * slots),
            transcendentals=0,
        ),
        name="source_rows",
    )(index[:, None, :], features, *pieces)


def edge_kernel(first, last, source_ref, basis_ref, owner_ref, w_in_ref, w_out_ref, *refs):
    out_ref = refs[-1]
    slots, width = source_ref.shape[1:]
    atoms = out_ref.shape[1]
    target = owner_ref[0, atoms : atoms + 1, first : first + slots].astype(jnp.float32)
    atom = lax.broadcasted_iota(jnp.int32, (atoms, slots), 0).astype(jnp.float32)
    incidence = jnp.where(atom == target, 1.0, 0.0)
    target_rows = jnp.dot(
        lax.transpose(incidence, (1, 0)).astype(jnp.bfloat16),
        owner_ref[0, :atoms],
        preferred_element_type=jnp.float32,
    ).astype(jnp.bfloat16)
    pre = jnp.dot(source_ref[0], w_in_ref[:width], preferred_element_type=jnp.float32)
    pre += jnp.dot(target_rows, w_in_ref[width : 2 * width], preferred_element_type=jnp.float32)
    pre += jnp.dot(basis_ref[0], w_in_ref[2 * width :], preferred_element_type=jnp.float32)
    half = 0.5 * pre
    hidden = (half + half * jnp.tanh(half)).astype(jnp.bfloat16)
    message = jnp.dot(hidden, w_out_ref[...], preferred_element_type=jnp.float32)
    total = jnp.dot(
        incidence.astype(jnp.bfloat16),
        message.astype(jnp.bfloat16),
        preferred_element_type=jnp.float32,
    )
    if first:
        total += refs[0][0]
    out_ref[0] = total.astype(out_ref.dtype)


def edge_network(source, basis, owners, w_in, w_out, first, last, before):
    groups, slots, width = source.shape
    atoms = owners.shape[1] - 16
    hidden = w_out.shape[0]
    block = pl.BlockSpec((1, atoms, width), lambda g: (g, 0, 0))
    part = first // slots
    return pl.pallas_call(
        functools.partial(edge_kernel, first, last),
        grid=(groups,),
        in_specs=[
            pl.BlockSpec((1, slots, width), lambda g: (g, 0, 0)),
            pl.BlockSpec((1, slots, basis.shape[2]), lambda g: (g, part, 0)),
            pl.BlockSpec((1, owners.shape[1], width), lambda g: (g, 0, 0)),
            pl.BlockSpec(w_in.shape, lambda g: (0, 0)),
            pl.BlockSpec(w_out.shape, lambda g: (0, 0)),
        ]
        + [block] * len(before),
        out_specs=block,
        out_shape=jax.ShapeDtypeStruct(
            (groups, atoms, width), jnp.bfloat16 if last else jnp.float32
        ),
        compiler_params=pltpu.CompilerParams(vmem_limit_bytes=VMEM_BYTES),
        cost_estimate=pl.CostEstimate(
            flops=2 * groups * slots * hidden * (w_in.shape[0] + width),
            bytes_accessed=2 * (groups * slots * w_in.shape[0] + w_in.size + w_out.size),
            transcendentals=groups * slots * hidden,
        ),
        name="edge_network",
    )(source, basis, owners, w_in, w_out, *before)


def place_kernel(odd_ref, *refs):
    pieces, (out_ref, sems) = refs[:PIECES], refs[PIECES:]
    low = 17 * odd_ref[0]
    copies = []
    for n, piece in enumerate(pieces):
        column, turn = divmod(n, 3)
        b = (1, 0, 2)[turn]
        if n == 0:
            for c in (0, 2):
                copies.append((piece.at[pl.ds(c, 1)], out_ref.at[pl.ds(12 + c // 2, 1)]))
        else:
            if column == 0:
                start = 9 if b == 0 else 14
            else:
                start = 3 * b + (low if column == 1 else 17 - low)
            copies.append((piece, out_ref.at[pl.ds(start, 3)]))
    copies = [
        pltpu.make_async_copy(here, there, sems.at[i]) for i, (here, there) in enumerate(copies)
    ]
    for copy in copies:
        copy.start()
    for copy in copies:
        copy.wait()


def placed(pieces, odd):
    shape = pieces[0].shape
    anywhere = pl.BlockSpec(memory_space=pl.ANY)
    return pl.pallas_call(
        place_kernel,
        in_specs=[pl.BlockSpec(memory_space=pltpu.SMEM)] + [anywhere] * PIECES,
        out_specs=anywhere,
        out_shape=jax.ShapeDtypeStruct((26, *shape[1:]), pieces[0].dtype),
        scratch_shapes=[pltpu.SemaphoreType.DMA((PIECES + 1,))],
        name="place_blocks",
    )(odd.astype(jnp.int32)[None], *pieces)


def exchange(x):
    return lax.all_to_all(x, "gz", split_axis=0, concat_axis=0, tiled=True)


def shards(
    features,
    halo_index,
    edge_src,
    edge_dst,
    edge_count,
    edge_basis,
    w_edge_in,
    w_edge_out,
    w_update,
):
    atoms, width = features.shape
    groups, slots = edge_src.shape
    halo_count = halo_index.shape[0]
    odd = lax.axis_index("gx") % 2 == 1
    basis = exchange(edge_basis.reshape(groups, slots, -1))

    slot_index = lax.broadcasted_iota(jnp.int32, (groups, slots), 1)
    live = slot_index < edge_count[:, None]
    target = jnp.where(live, edge_dst, -1).astype(features.dtype)
    target = jnp.pad(target[:, None, :], ((0, 0), (0, 15), (0, width - slots)))
    copies = jnp.broadcast_to(features, (groups, atoms, width))
    owners = exchange(jnp.concatenate([copies, target], axis=1))

    pieces = halo_pieces(features[halo_index])
    index = table_row(edge_src, atoms, halo_count, odd)
    half = slots // 2
    source_0 = exchange(gather_rows(index[:, :half], features, pieces))
    source_1 = exchange(gather_rows(index[:, half:], features, pieces))
    network = functools.partial(
        edge_network, basis=basis, owners=owners, w_in=w_edge_in[0], w_out=w_edge_out[0]
    )
    partial_sums = network(source_0, first=0, last=False, before=())
    partial_sums = network(source_1, first=half, last=True, before=(partial_sums,))

    summed = jnp.sum(exchange(partial_sums).astype(jnp.float32), axis=0)
    mean_square = jnp.mean(summed * summed, axis=-1, keepdims=True)
    normed = (summed * lax.rsqrt(mean_square + 1e-05)).astype(jnp.bfloat16)
    update = jnp.dot(normed, w_update, preferred_element_type=jnp.float32)
    new_rows = (features.astype(jnp.float32) + update).astype(jnp.bfloat16)
    return new_rows, placed(halo_pieces(new_rows[halo_index]), odd)


def solution(mesh):
    everywhere = ("gx", "gy", "gz")
    in_specs = (
        P(everywhere, None),
        P(everywhere),
        P(everywhere, None),
        P(everywhere, None),
        P(everywhere),
        P(everywhere, None),
        P("gz", None, None),
        P("gz", None, None),
        P(),
    )
    out_specs = (P(everywhere, None), P(everywhere, None, None))
    return jax.shard_map(shards, mesh=mesh, in_specs=in_specs, out_specs=out_specs, check_vma=False)
```

time: 244 us -> 272 us (1.11); the launches traced: 239 us -> 272 us
  Pallas kernels: 0 us -> 126 us
  matrix products: 35.8 us -> 0.27 us
  blocking collectives: 44.8 us -> 18.1 us
  local copies, waits for them, and re-layouts: 32.7 us -> 6.93 us
  starting transfers between devices: 43.9 us -> 50.9 us
  waiting for transfers between devices: 73.1 us -> 66.5 us
  other arithmetic: 8.03 us -> 1.64 us
    pallas_call x0 -> x5, Pallas kernels: none -> 126 us  [the longest x1 78.6 us: placed(): pl.pallas_call(place_kernel, in_specs=[pl.BlockSpec(memory_space=pltpu.SM...]
    dot_general x4 -> x0, matrix products: 35.6 us -> none  [the longest x1 12.7 us: shards(): jnp.einsum('och,hd->ocd', hidden, w_second, preferred_element_type=jnp.fl...]
    gather x4 -> x2, local copies, waits for them, and re-layouts: 31.3 us -> 1.55 us  [the longest x1 0.78 us: shards(): pieces = halo_pieces(features[halo_index])]
    all_to_all x2 -> x1, blocking collectives: 44.8 us -> 18.1 us  [exchange(): return lax.all_to_all(x, 'gz', split_axis=0, concat_axis=0, tiled=True)]
    all_to_all x3 -> x4, waiting for transfers between devices: 36.4 us -> 27 us  [exchange(): return lax.all_to_all(x, 'gz', split_axis=0, concat_axis=0, tiled=True)]
    all_to_all x3 -> x4, starting transfers between devices: 12.5 us -> 18.7 us  [exchange(): return lax.all_to_all(x, 'gz', split_axis=0, concat_axis=0, tiled=True)]
    concatenate x9 -> x1, other arithmetic: 6.77 us -> 1.18 us  [shards(): owners = exchange(jnp.concatenate([copies, target], axis=1))]
    unnamed x17 -> x58, local copies, waits for them, and re-layouts: 0.06 us -> 4 us
  transfers between devices with their start and end apart: 15 -> 24, of which waited for: 10 -> 12; matrix products, arithmetic and copies ran while one was open for 23% -> 1% of each run, Pallas kernels for 0% -> 12%
where the time goes in v1:
time: 272 us
  Pallas kernels  126 us (46%)
  waiting for transfers between devices  66.5 us (24%)
  starting transfers between devices  50.9 us (19%)
  blocking collectives  18.1 us (7%)
  local copies, waits for them, and re-layouts  6.93 us (3%)
    pallas_call x1, Pallas kernels, placed(): pl.pallas_call(place_kernel, in_specs=[pl.BlockSpec(memory_space=pltpu.SM...  78.6 us
    pallas_call x2, Pallas kernels, edge_network(): pl.pallas_call(functools.partial(edge_kernel, first, last), grid=(groups,...  28.1 us
    all_to_all x4, waiting for transfers between devices, exchange(): return lax.all_to_all(x, 'gz', split_axis=0, concat_axis=0, tiled=True)  27 us
    ppermute x6, waiting for transfers between devices, from_before(): return lax.ppermute(x, axis, ring(axis, 1))  21.1 us
    pallas_call x2, Pallas kernels, gather_rows(): pl.pallas_call(gather_kernel, grid=(groups,), in_specs=[pl.BlockSpec((1,...  19.6 us
    all_to_all x4, starting transfers between devices, exchange(): return lax.all_to_all(x, 'gz', split_axis=0, concat_axis=0, tiled=True)  18.7 us
    all_to_all x1, blocking collectives, exchange(): return lax.all_to_all(x, 'gz', split_axis=0, concat_axis=0, tiled=True)  18.1 us
    ppermute x2, starting transfers between devices, outer_swap(): return lax.ppermute(x, 'gx', pairs)  11.9 us
  transfers between devices with their start and end apart: 24, of which 12 were waited for; matrix products, arithmetic and copies ran while one was open for 1% of the time, Pallas kernels for 12%

profile of v1, /device:TPU:1, one launch (start us, length us, event | category | flops | bytes accessed | tf_op | source)
XLA Modules:
  0.0 271.8 jit_solution(11908777233568703696)
XLA Ops:
  0.7 6.3 %all-to-all-start.1 = ((bf16[8,384,128]{2,1,0:T(8,128)(2,1)}), bf16[8,384,128]{2,1,0:T(8,128)(2,1)S(1)}, u32[]{:S(2)}, u32[]{:S(2)}) async-start(bf16[8,384,128]{2,1,0:T(8,128)(2,1)} %bitcast.24), calls=%async_computation.1 | async-start | bytes 1572864 | tf_op jit(solution)/shard_map/all_to_all | solution.py:220
  8.4 10.0 %all-to-all-done.1.basis_ref = bf16[8,384,128]{2,1,0:T(8,128)(2,1)S(1)} async-done(((bf16[8,384,128]{2,1,0:T(8,128)(2,1)}), bf16[8,384,128]{2,1,0:T(8,128)(2,1)S(1)}, u32[]{:S(2)}, u32[]{:S(2)}) %all-to-all-start.1) | async-done | bytes 786464 | tf_op jit(solution)/shard_map/all_to_all | solution.py:220
  18.4 4.4 %all-to-all-start.2 = ((bf16[8,144,512]{2,1,0:T(8,128)(2,1)}), bf16[8,144,512]{2,1,0:T(8,128)(2,1)S(1)}, u32[]{:S(2)}, u32[]{:S(2)}) async-start(bf16[8,144,512]{2,1,0:T(8,128)(2,1)} %fusion.1), calls=%async_computation.2 | async-start | bytes 2359296 | tf_op jit(solution)/shard_map/all_to_all | solution.py:220
  27.4 13.7 %collective-permute-done = bf16[96,512]{1,0:T(8,128)(2,1)S(1)} collective-permute-done((bf16[96,512]{1,0:T(8,128)(2,1)S(1)}, bf16[96,512]{1,0:T(8,128)(2,1)S(1)}, u32[]{:S(2)}, u32[]{:S(2)}) %collective-permute-start) | collective-permute-done | bytes 98336 | tf_op jit(solution)/shard_map/ppermute | solution.py:20
  41.2 4.9 %collective-permute-start.4 = (bf16[3,96,512]{2,1,0:T(8,128)(2,1)S(1)}, bf16[3,96,512]{2,1,0:T(8,128)(2,1)S(1)}, u32[]{:S(2)}, u32[]{:S(2)}) collective-permute-start(bf16[3,96,512]{2,1,0:T(8,128)(2,1)S(1)} %pad_maximum_fusion), channel_id=1, source_target_pairs={{0,224},{32,64},{64,32},{96,128},{128,96},{160,192},{192,160},{224... | collective-permute-start | bytes 884744 | tf_op jit(solution)/shard_map/ppermute | solution.py:35
  46.1 2.7 %collective-permute-start.3 = (bf16[3,96,512]{2,1,0:T(8,128)(2,1)S(1)}, bf16[3,96,512]{2,1,0:T(8,128)(2,1)S(1)}, u32[]{:S(2)}, u32[]{:S(2)}) collective-permute-start(bf16[3,96,512]{2,1,0:T(8,128)(2,1)S(1)} %pad_maximum_fusion), channel_id=1, source_target_pairs={{0,24},{8,0},{16,8},{24,16},{1,25},{9,1},{17,9},{25,17},{2,26},{10... | collective-permute-start | bytes 884744 | tf_op jit(solution)/shard_map/ppermute | solution.py:24
  49.8 3.9 %collective-permute-done.4 = bf16[3,96,512]{2,1,0:T(8,128)(2,1)S(1)} collective-permute-done((bf16[3,96,512]{2,1,0:T(8,128)(2,1)S(1)}, bf16[3,96,512]{2,1,0:T(8,128)(2,1)S(1)}, u32[]{:S(2)}, u32[]{:S(2)}) %collective-permute-start.4) | collective-permute-done | bytes 294944 | tf_op jit(solution)/shard_map/ppermute | solution.py:35
  53.7 3.0 %collective-permute-start.6 = (bf16[3,96,512]{2,1,0:T(8,128)(2,1)S(1)}, bf16[3,96,512]{2,1,0:T(8,128)(2,1)S(1)}, u32[]{:S(2)}, u32[]{:S(2)}) collective-permute-start(bf16[3,96,512]{2,1,0:T(8,128)(2,1)S(1)} %collective-permute-done.4), channel_id=1, source_target_pairs={{0,24},{8,0},{16,8},{24,16},{1,25},{9,1},{17,9},{25,17},{2,26},{10... | collective-permute-start | bytes 884744 | tf_op jit(solution)/shard_map/ppermute | solution.py:24
  60.2 2.7 collective-permute-done.6
  62.9 3.4 %collective-permute-done.5 = bf16[3,96,512]{2,1,0:T(8,128)(2,1)S(1)} collective-permute-done((bf16[3,96,512]{2,1,0:T(8,128)(2,1)S(1)}, bf16[3,96,512]{2,1,0:T(8,128)(2,1)S(1)}, u32[]{:S(2)}, u32[]{:S(2)}) %collective-permute-start.5) | collective-permute-done | bytes 294944 | tf_op jit(solution)/shard_map/ppermute | solution.py:20
  67.2 9.8 %source_rows.3 = bf16[8,192,512]{2,1,0:T(8,128)(2,1)} custom-call(s32[8,1,192]{2,1,0:T(1,128)} %broadcast_in_dim.41.index_ref, bf16[128,512]{1,0:T(8,128)(2,1)} %features_ref.3, bf16[288,512]{1,0:T(8,128)(2,1)} %bitcast.27, bf16[288,512]{1,0:T(8,128)(2,1)} %bitcast.41, bf16[288,512]{1,0:T(8,128)(2,1)} %bitcast.39, bf16[288,512]{1,0:T(8,128)(2,1)} %bitcast.37, ...), custom_call_target="tpu_custom_call" | custom-call | flops 4429185024 | bytes 4456448 | tf_op jit(solution)/shard_map/source_rows/pallas_call | solution.py:101
  78.1 3.6 %all-to-all-start.3 = ((bf16[8,192,512]{2,1,0:T(8,128)(2,1)}), bf16[8,192,512]{2,1,0:T(8,128)(2,1)S(1)}, u32[]{:S(2)}, u32[]{:S(2)}) async-start(bf16[8,192,512]{2,1,0:T(8,128)(2,1)} %source_rows.3), calls=%async_computation.3 | async-start | bytes 3145728 | tf_op jit(solution)/shard_map/all_to_all | solution.py:220
  82.3 9.8 %source_rows.2 = bf16[8,192,512]{2,1,0:T(8,128)(2,1)} custom-call(s32[8,1,192]{2,1,0:T(1,128)} %copy.15.index_ref, bf16[128,512]{1,0:T(8,128)(2,1)} %features_ref.3, bf16[288,512]{1,0:T(8,128)(2,1)} %bitcast.28, bf16[288,512]{1,0:T(8,128)(2,1)} %bitcast.42, bf16[288,512]{1,0:T(8,128)(2,1)} %bitcast.40, bf16[288,512]{1,0:T(8,128)(2,1)} %bitcast.38, ...), custom_call_target="tpu_custom_call" | custom-call | flops 4429185024 | bytes 4456448 | tf_op jit(solution)/shard_map/source_rows/pallas_call | solution.py:101
  92.1 10.1 %all-to-all-done.3.source_ref = bf16[8,192,512]{2,1,0:T(8,128)(2,1)S(1)} async-done(((bf16[8,192,512]{2,1,0:T(8,128)(2,1)}), bf16[8,192,512]{2,1,0:T(8,128)(2,1)S(1)}, u32[]{:S(2)}, u32[]{:S(2)}) %all-to-all-start.3) | async-done | bytes 1572896 | tf_op jit(solution)/shard_map/all_to_all | solution.py:220
  103.3 4.3 %all-to-all-start = ((bf16[8,192,512]{2,1,0:T(8,128)(2,1)}), bf16[8,192,512]{2,1,0:T(8,128)(2,1)}, u32[]{:S(2)}, u32[]{:S(2)}) async-start(bf16[8,192,512]{2,1,0:T(8,128)(2,1)} %source_rows.2), calls=%async_computation | async-start | bytes 3145728 | tf_op jit(solution)/shard_map/all_to_all | solution.py:220
  107.6 13.7 %edge_network.2.refs_0_ = f32[8,128,512]{2,1,0:T(8,128)} custom-call(bf16[8,192,512]{2,1,0:T(8,128)(2,1)} %copy-done.4, bf16[8,384,128]{2,1,0:T(8,128)(2,1)} %copy-done.7, bf16[8,144,512]{2,1,0:T(8,128)(2,1)} %copy-done.5, bf16[1152,1024]{1,0:T(8,128)(2,1)} %bitcast.33, bf16[1024,512]{1,0:T(8,128)(2,1)} %bitcast.35), custom_call_target="tpu_custom_call" | custom-call | flops 5234491392 | bytes 6946816 | tf_op jit(solution)/shard_map/edge_network/pallas_call | solution.py:156
  121.4 6.8 %all-to-all-done.source_ref = bf16[8,192,512]{2,1,0:T(8,128)(2,1)} async-done(((bf16[8,192,512]{2,1,0:T(8,128)(2,1)}), bf16[8,192,512]{2,1,0:T(8,128)(2,1)}, u32[]{:S(2)}, u32[]{:S(2)}) %all-to-all-start) | async-done | bytes 1572896 | tf_op jit(solution)/shard_map/all_to_all | solution.py:220
  128.2 14.4 %edge_network.3 = bf16[8,128,512]{2,1,0:T(8,128)(2,1)} custom-call(bf16[8,192,512]{2,1,0:T(8,128)(2,1)} %all-to-all-done.source_ref, bf16[8,384,128]{2,1,0:T(8,128)(2,1)} %copy-done.7, bf16[8,144,512]{2,1,0:T(8,128)(2,1)} %copy-done.5, bf16[1152,1024]{1,0:T(8,128)(2,1)} %bitcast.34, bf16[1024,512]{1,0:T(8,128)(2,1)} %bitcast.36, ...), custom_call_target="tpu_custom_call" | custom-call | flops 5234491392 | bytes 6946816 | tf_op jit(solution)/shard_map/edge_network/pallas_call | solution.py:156
  142.6 18.1 %all_to_all.25 = bf16[8,128,512]{2,1,0:T(8,128)(2,1)S(1)} all-to-all(bf16[8,128,512]{2,1,0:T(8,128)(2,1)} %edge_network.3), channel_id=1, replica_groups=mesh['gx'=8,'gy'=4,'gz'=8] {'gz'}, dimensions={0} | all-to-all | bytes 2097152 | tf_op jit(solution)/shard_map/all_to_all | solution.py:220
  162.4 3.6 %collective-permute-start.11 = (bf16[96,512]{1,0:T(8,128)(2,1)S(1)}, bf16[96,512]{1,0:T(8,128)(2,1)S(1)}, u32[]{:S(2)}, u32[]{:S(2)}) collective-permute-start(bf16[96,512]{1,0:T(8,128)(2,1)S(1)} %gather_fusion.1), channel_id=1, source_target_pairs={{0,7},{1,0},{2,1},{3,2},{4,3},{5,4},{6,5},{7,6},{8,15},{9,8},{10,9... | collective-permute-start | bytes 294920 | tf_op jit(solution)/shard_map/ppermute | solution.py:24
  168.0 7.1 %collective-permute-start.14 = (bf16[3,96,512]{2,1,0:T(8,128)(2,1)S(1)}, bf16[3,96,512]{2,1,0:T(8,128)(2,1)S(1)}, u32[]{:S(2)}, u32[]{:S(2)}) collective-permute-start(bf16[3,96,512]{2,1,0:T(8,128)(2,1)S(1)} %pad_maximum_fusion.1.refs_0_), channel_id=1, source_target_pairs={{0,224},{32,64},{64,32},{96,128},{128,96},{160,192},{192,160},{224... | collective-permute-start | bytes 884744 | tf_op jit(solution)/shard_map/ppermute | solution.py:35
  176.6 6.1 %collective-permute-done.14.refs_3_ = bf16[3,96,512]{2,1,0:T(8,128)(2,1)S(1)} collective-permute-done((bf16[3,96,512]{2,1,0:T(8,128)(2,1)S(1)}, bf16[3,96,512]{2,1,0:T(8,128)(2,1)S(1)}, u32[]{:S(2)}, u32[]{:S(2)}) %collective-permute-start.14) | collective-permute-done | bytes 294944 | tf_op jit(solution)/shard_map/ppermute | solution.py:35
  185.2 5.7 %collective-permute-done.16.refs_5_ = bf16[3,96,512]{2,1,0:T(8,128)(2,1)S(1)} collective-permute-done((bf16[3,96,512]{2,1,0:T(8,128)(2,1)S(1)}, bf16[3,96,512]{2,1,0:T(8,128)(2,1)S(1)}, u32[]{:S(2)}, u32[]{:S(2)}) %collective-permute-start.16) | collective-permute-done | bytes 294944 | tf_op jit(solution)/shard_map/ppermute | solution.py:24
  193.0 78.6 %place_blocks.1 = bf16[26,96,512]{2,1,0:T(8,128)(2,1)} custom-call(s32[1]{0:T(128)} %bitcast.17.odd_ref, bf16[3,96,512]{2,1,0:T(8,128)(2,1)} %copy-done.6, bf16[3,96,512]{2,1,0:T(8,128)(2,1)} %copy-done.11, bf16[3,96,512]{2,1,0:T(8,128)(2,1)} %copy-done.10, bf16[3,96,512]{2,1,0:T(8,128)(2,1)} %copy-done.9, bf16[3,96,512]{2,1,0:T(8,128)(2,1)} %copy-done.14, ...), custom_call_target="tpu_custom_call" | custom-call | tf_op jit(solution)/shard_map/place_blocks/pallas_call | solution.py:209
  (106 shorter events, 23.8 us)
Async XLA Ops:
  0.7 17.7 %all-to-all-start.1 = ((bf16[8,384,128]{2,1,0:T(8,128)(2,1)}), bf16[8,384,128]{2,1,0:T(8,128)(2,1)S(1)}, u32[]{:S(2)}, u32[]{:S(2)}) async-start(bf16[8,384,128]{2,1,0:T(8,128)(2,1)} %bitcast.24), calls=%async_computation.1 | async-start | bytes 1572864 | tf_op jit(solution)/shard_map/all_to_all | solution.py:220
  18.4 58.6 %all-to-all-start.2 = ((bf16[8,144,512]{2,1,0:T(8,128)(2,1)}), bf16[8,144,512]{2,1,0:T(8,128)(2,1)S(1)}, u32[]{:S(2)}, u32[]{:S(2)}) async-start(bf16[8,144,512]{2,1,0:T(8,128)(2,1)} %fusion.1), calls=%async_computation.2 | async-start | bytes 2359296 | tf_op jit(solution)/shard_map/all_to_all | solution.py:220
  23.7 17.5 %collective-permute-start = (bf16[96,512]{1,0:T(8,128)(2,1)S(1)}, bf16[96,512]{1,0:T(8,128)(2,1)S(1)}, u32[]{:S(2)}, u32[]{:S(2)}) collective-permute-start(bf16[96,512]{1,0:T(8,128)(2,1)S(1)} %gather_fusion), channel_id=1, source_target_pairs={{0,1},{1,2},{2,3},{3,4},{4,5},{5,6},{6,7},{7,0},{8,9},{9,10},{10,1... | collective-permute-start | bytes 294920 | tf_op jit(solution)/shard_map/ppermute | solution.py:20
  25.2 16.0 %collective-permute-start.1 = (bf16[96,512]{1,0:T(8,128)(2,1)S(1)}, bf16[96,512]{1,0:T(8,128)(2,1)S(1)}, u32[]{:S(2)}, u32[]{:S(2)}) collective-permute-start(bf16[96,512]{1,0:T(8,128)(2,1)S(1)} %gather_fusion), channel_id=1, source_target_pairs={{0,7},{1,0},{2,1},{3,2},{4,3},{5,4},{6,5},{7,6},{8,15},{9,8},{10,9... | collective-permute-start | bytes 294920 | tf_op jit(solution)/shard_map/ppermute | solution.py:24
  41.2 12.5 %collective-permute-start.4 = (bf16[3,96,512]{2,1,0:T(8,128)(2,1)S(1)}, bf16[3,96,512]{2,1,0:T(8,128)(2,1)S(1)}, u32[]{:S(2)}, u32[]{:S(2)}) collective-permute-start(bf16[3,96,512]{2,1,0:T(8,128)(2,1)S(1)} %pad_maximum_fusion), channel_id=1, source_target_pairs={{0,224},{32,64},{64,32},{96,128},{128,96},{160,192},{192,160},{224... | collective-permute-start | bytes 884744 | tf_op jit(solution)/shard_map/ppermute | solution.py:35
  46.1 10.6 %collective-permute-start.3 = (bf16[3,96,512]{2,1,0:T(8,128)(2,1)S(1)}, bf16[3,96,512]{2,1,0:T(8,128)(2,1)S(1)}, u32[]{:S(2)}, u32[]{:S(2)}) collective-permute-start(bf16[3,96,512]{2,1,0:T(8,128)(2,1)S(1)} %pad_maximum_fusion), channel_id=1, source_target_pairs={{0,24},{8,0},{16,8},{24,16},{1,25},{9,1},{17,9},{25,17},{2,26},{10... | collective-permute-start | bytes 884744 | tf_op jit(solution)/shard_map/ppermute | solution.py:24
  48.8 8.7 %collective-permute-start.2 = (bf16[3,96,512]{2,1,0:T(8,128)(2,1)S(1)}, bf16[3,96,512]{2,1,0:T(8,128)(2,1)S(1)}, u32[]{:S(2)}, u32[]{:S(2)}) collective-permute-start(bf16[3,96,512]{2,1,0:T(8,128)(2,1)S(1)} %pad_maximum_fusion), channel_id=1, source_target_pairs={{0,8},{8,16},{16,24},{24,0},{1,9},{9,17},{17,25},{25,1},{2,10},{10... | collective-permute-start | bytes 884744 | tf_op jit(solution)/shard_map/ppermute | solution.py:20
  48.8 11.4 %collective-permute-start.7 = (bf16[3,96,512]{2,1,0:T(8,128)(2,1)S(1)}, bf16[3,96,512]{2,1,0:T(8,128)(2,1)S(1)}, u32[]{:S(2)}, u32[]{:S(2)}) collective-permute-start(bf16[3,96,512]{2,1,0:T(8,128)(2,1)S(1)} %pad_maximum_fusion), channel_id=1, source_target_pairs={{0,32},{32,0},{64,96},{96,64},{128,160},{160,128},{192,224},{224,1... | collective-permute-start | bytes 884744 | tf_op jit(solution)/shard_map/ppermute | solution.py:29
  53.7 9.2 %collective-permute-start.6 = (bf16[3,96,512]{2,1,0:T(8,128)(2,1)S(1)}, bf16[3,96,512]{2,1,0:T(8,128)(2,1)S(1)}, u32[]{:S(2)}, u32[]{:S(2)}) collective-permute-start(bf16[3,96,512]{2,1,0:T(8,128)(2,1)S(1)} %collective-permute-done.4), channel_id=1, source_target_pairs={{0,24},{8,0},{16,8},{24,16},{1,25},{9,1},{17,9},{25,17},{2,26},{10... | collective-permute-start | bytes 884744 | tf_op jit(solution)/shard_map/ppermute | solution.py:24
  56.7 9.6 %collective-permute-start.5 = (bf16[3,96,512]{2,1,0:T(8,128)(2,1)S(1)}, bf16[3,96,512]{2,1,0:T(8,128)(2,1)S(1)}, u32[]{:S(2)}, u32[]{:S(2)}) collective-permute-start(bf16[3,96,512]{2,1,0:T(8,128)(2,1)S(1)} %collective-permute-done.4), channel_id=1, source_target_pairs={{0,8},{8,16},{16,24},{24,0},{1,9},{9,17},{17,25},{25,1},{2,10},{10... | collective-permute-start | bytes 884744 | tf_op jit(solution)/shard_map/ppermute | solution.py:20
  56.7 9.6 %collective-permute-start.9 = (bf16[3,96,512]{2,1,0:T(8,128)(2,1)S(1)}, bf16[3,96,512]{2,1,0:T(8,128)(2,1)S(1)}, u32[]{:S(2)}, u32[]{:S(2)}) collective-permute-start(bf16[3,96,512]{2,1,0:T(8,128)(2,1)S(1)} %collective-permute-done.3), channel_id=1, source_target_pairs={{0,32},{32,0},{64,96},{96,64},{128,160},{160,128},{192,224},{224,1... | collective-permute-start | bytes 884744 | tf_op jit(solution)/shard_map/ppermute | solution.py:29
  57.5 8.8 %collective-permute-start.8 = (bf16[3,96,512]{2,1,0:T(8,128)(2,1)S(1)}, bf16[3,96,512]{2,1,0:T(8,128)(2,1)S(1)}, u32[]{:S(2)}, u32[]{:S(2)}) collective-permute-start(bf16[3,96,512]{2,1,0:T(8,128)(2,1)S(1)} %collective-permute-done.2), channel_id=1, source_target_pairs={{0,32},{32,0},{64,96},{96,64},{128,160},{160,128},{192,224},{224,1... | collective-permute-start | bytes 884744 | tf_op jit(solution)/shard_map/ppermute | solution.py:29
  78.1 24.1 %all-to-all-start.3 = ((bf16[8,192,512]{2,1,0:T(8,128)(2,1)}), bf16[8,192,512]{2,1,0:T(8,128)(2,1)S(1)}, u32[]{:S(2)}, u32[]{:S(2)}) async-start(bf16[8,192,512]{2,1,0:T(8,128)(2,1)} %source_rows.3), calls=%async_computation.3 | async-start | bytes 3145728 | tf_op jit(solution)/shard_map/all_to_all | solution.py:220
  103.3 24.9 %all-to-all-start = ((bf16[8,192,512]{2,1,0:T(8,128)(2,1)}), bf16[8,192,512]{2,1,0:T(8,128)(2,1)}, u32[]{:S(2)}, u32[]{:S(2)}) async-start(bf16[8,192,512]{2,1,0:T(8,128)(2,1)} %source_rows.2), calls=%async_computation | async-start | bytes 3145728 | tf_op jit(solution)/shard_map/all_to_all | solution.py:220
  162.1 5.8 %collective-permute-start.10 = (bf16[96,512]{1,0:T(8,128)(2,1)S(1)}, bf16[96,512]{1,0:T(8,128)(2,1)S(1)}, u32[]{:S(2)}, u32[]{:S(2)}) collective-permute-start(bf16[96,512]{1,0:T(8,128)(2,1)S(1)} %gather_fusion.1), channel_id=1, source_target_pairs={{0,1},{1,2},{2,3},{3,4},{4,5},{5,6},{6,7},{7,0},{8,9},{9,10},{10,1... | collective-permute-start | bytes 294920 | tf_op jit(solution)/shard_map/ppermute | solution.py:20
  162.4 5.6 %collective-permute-start.11 = (bf16[96,512]{1,0:T(8,128)(2,1)S(1)}, bf16[96,512]{1,0:T(8,128)(2,1)S(1)}, u32[]{:S(2)}, u32[]{:S(2)}) collective-permute-start(bf16[96,512]{1,0:T(8,128)(2,1)S(1)} %gather_fusion.1), channel_id=1, source_target_pairs={{0,7},{1,0},{2,1},{3,2},{4,3},{5,4},{6,5},{7,6},{8,15},{9,8},{10,9... | collective-permute-start | bytes 294920 | tf_op jit(solution)/shard_map/ppermute | solution.py:24
  168.0 14.6 %collective-permute-start.14 = (bf16[3,96,512]{2,1,0:T(8,128)(2,1)S(1)}, bf16[3,96,512]{2,1,0:T(8,128)(2,1)S(1)}, u32[]{:S(2)}, u32[]{:S(2)}) collective-permute-start(bf16[3,96,512]{2,1,0:T(8,128)(2,1)S(1)} %pad_maximum_fusion.1.refs_0_), channel_id=1, source_target_pairs={{0,224},{32,64},{64,32},{96,128},{128,96},{160,192},{192,160},{224... | collective-permute-start | bytes 884744 | tf_op jit(solution)/shard_map/ppermute | solution.py:35
  175.1 9.0 %collective-permute-start.13 = (bf16[3,96,512]{2,1,0:T(8,128)(2,1)S(1)}, bf16[3,96,512]{2,1,0:T(8,128)(2,1)S(1)}, u32[]{:S(2)}, u32[]{:S(2)}) collective-permute-start(bf16[3,96,512]{2,1,0:T(8,128)(2,1)S(1)} %pad_maximum_fusion.1.refs_0_), channel_id=1, source_target_pairs={{0,24},{8,0},{16,8},{24,16},{1,25},{9,1},{17,9},{25,17},{2,26},{10... | collective-permute-start | bytes 884744 | tf_op jit(solution)/shard_map/ppermute | solution.py:24
  175.1 10.0 %collective-permute-start.12 = (bf16[3,96,512]{2,1,0:T(8,128)(2,1)S(1)}, bf16[3,96,512]{2,1,0:T(8,128)(2,1)S(1)}, u32[]{:S(2)}, u32[]{:S(2)}) collective-permute-start(bf16[3,96,512]{2,1,0:T(8,128)(2,1)S(1)} %pad_maximum_fusion.1.refs_0_), channel_id=1, source_target_pairs={{0,8},{8,16},{16,24},{24,0},{1,9},{9,17},{17,25},{25,1},{2,10},{10... | collective-permute-start | bytes 884744 | tf_op jit(solution)/shard_map/ppermute | solution.py:20
  176.6 8.6 %collective-permute-start.17 = (bf16[3,96,512]{2,1,0:T(8,128)(2,1)S(1)}, bf16[3,96,512]{2,1,0:T(8,128)(2,1)S(1)}, u32[]{:S(2)}, u32[]{:S(2)}) collective-permute-start(bf16[3,96,512]{2,1,0:T(8,128)(2,1)S(1)} %pad_maximum_fusion.1.refs_0_), channel_id=1, source_target_pairs={{0,32},{32,0},{64,96},{96,64},{128,160},{160,128},{192,224},{224,1... | collective-permute-start | bytes 884744 | tf_op jit(solution)/shard_map/ppermute | solution.py:29
  182.7 8.2 %collective-permute-start.16 = (bf16[3,96,512]{2,1,0:T(8,128)(2,1)S(1)}, bf16[3,96,512]{2,1,0:T(8,128)(2,1)S(1)}, u32[]{:S(2)}, u32[]{:S(2)}) collective-permute-start(bf16[3,96,512]{2,1,0:T(8,128)(2,1)S(1)} %collective-permute-done.14.refs_3_), channel_id=1, source_target_pairs={{0,24},{8,0},{16,8},{24,16},{1,25},{9,1},{17,9},{25,17},{2,26},{10... | collective-permute-start | bytes 884744 | tf_op jit(solution)/shard_map/ppermute | solution.py:24
  182.7 9.4 %collective-permute-start.15 = (bf16[3,96,512]{2,1,0:T(8,128)(2,1)S(1)}, bf16[3,96,512]{2,1,0:T(8,128)(2,1)S(1)}, u32[]{:S(2)}, u32[]{:S(2)}) collective-permute-start(bf16[3,96,512]{2,1,0:T(8,128)(2,1)S(1)} %collective-permute-done.14.refs_3_), channel_id=1, source_target_pairs={{0,8},{8,16},{16,24},{24,0},{1,9},{9,17},{17,25},{25,1},{2,10},{10... | collective-permute-start | bytes 884744 | tf_op jit(solution)/shard_map/ppermute | solution.py:20
  184.1 8.0 %collective-permute-start.19 = (bf16[3,96,512]{2,1,0:T(8,128)(2,1)S(1)}, bf16[3,96,512]{2,1,0:T(8,128)(2,1)S(1)}, u32[]{:S(2)}, u32[]{:S(2)}) collective-permute-start(bf16[3,96,512]{2,1,0:T(8,128)(2,1)S(1)} %collective-permute-done.13.refs_2_), channel_id=1, source_target_pairs={{0,32},{32,0},{64,96},{96,64},{128,160},{160,128},{192,224},{224,1... | collective-permute-start | bytes 884744 | tf_op jit(solution)/shard_map/ppermute | solution.py:29
  185.1 7.0 %collective-permute-start.18 = (bf16[3,96,512]{2,1,0:T(8,128)(2,1)S(1)}, bf16[3,96,512]{2,1,0:T(8,128)(2,1)S(1)}, u32[]{:S(2)}, u32[]{:S(2)}) collective-permute-start(bf16[3,96,512]{2,1,0:T(8,128)(2,1)S(1)} %collective-permute-done.12.refs_1_), channel_id=1, source_target_pairs={{0,32},{32,0},{64,96},{96,64},{128,160},{160,128},{192,224},{224,1... | collective-permute-start | bytes 884744 | tf_op jit(solution)/shard_map/ppermute | solution.py:29
  (29 other events, 509.1 us)
